TPU v7x, 256 devices: a whole 4x4x8 slice. The times are simulated.
256 devices in a mesh: cell: 64 (over y, z, core), view: 4 (over x).
Axes of the slice: x: 4, y: 4, z: 8, core: 2. Of those that a mesh axis runs over, the one named last changes fastest.
Arguments:
- gaussians: float32 [1024, 9, 256], P('cell'), as said below
- seg_count: int32 [4, 64], P('view', 'cell'), may hold values from 1 to 3, as said below
- seg_block: int32 [4, 64, 3], P('view', 'cell'), may hold values from 0 to 1023, as said below
- ray_count: int32 [4, 64], P('view', 'cell'), may hold values from 576 to 2304
- camera_shift: float32 [4, 2], P('view'), may hold values from -6 to 6
- target: float32 [4, 64, 3, 2304], P('view', 'cell'), may hold values from 0 to 1
Outputs:
- image: float32 [4, 64, 3, 2304], P('view', 'cell')
- gauss_grad: float32 [1024, 9, 256], P('cell')
Inputs may be any that keep to these rules, and one draw needn't show every extreme that they name: `gaussians`: each column of a block is one Gaussian: a mean, the entries a, b, c of a positive definite inverse covariance, an opacity in (0, 1), three colours. `seg_count`: tiles 2m and 2m + 1 of a view hold 4 segments together; in every view some tile holds 3. Segment k of tile t uses a block stored in cell seg_block // 16, which is t + e modulo 64 for some e from -2 to 2; entries at k >= seg_count are not used.
All inputs are finite; a program needn't handle non-finite values.
Results may differ from a plain program's by a relative error of at most 0.0003.
Values sent between devices are 32-bit elements; how exact they have to be, the bound alone decides.
No kernel may reach another device: no remote copies, remote signals or barrier semaphores. Data moves between devices by JAX's collectives and lax.ppermute only.
A program may use at most 64 MiB of HBM per device.

v0:
```python
import jax
import jax.numpy as jnp
from jax import lax
from jax.sharding import PartitionSpec as P

TILE = 48
REACH = 2
precise = lax.Precision.HIGHEST


def shifted(block, axis, distance):
    devices = range(lax.axis_size(axis))
    route = [((i - distance) % len(devices), i) for i in devices]
    return lax.ppermute(block, axis, route)


def pixel_frame(shift, pixels):
    pixel_ids = jnp.arange(pixels)
    centre = (TILE - 1) / 2.0
    pix_x = (pixel_ids % TILE).astype(jnp.float32) - centre - shift[0]
    pix_y = (pixel_ids // TILE).astype(jnp.float32) - centre - shift[1]
    return (pix_x, pix_y)


def triangles(length):
    row_ids = lax.broadcasted_iota(jnp.int32, (length, length), 0)
    col_ids = lax.broadcasted_iota(jnp.int32, (length, length), 1)
    return ((col_ids < row_ids).astype(jnp.float32), (col_ids > row_ids).astype(jnp.float32))


def splat(params, pix_x, pix_y):
    delta_x = pix_x[None, :] - params[0][:, None]
    delta_y = pix_y[None, :] - params[1][:, None]
    quad_form = (
        params[2][:, None] * delta_x * delta_x
        + 2.0 * params[3][:, None] * delta_x * delta_y
        + params[4][:, None] * delta_y * delta_y
    )
    alphas = params[5][:, None] * jnp.exp(-0.5 * quad_form)
    return (alphas, jnp.log1p(-alphas))


def forward_task(params, pix_x, pix_y, lower_tri):
    alphas, log_trans = splat(params, pix_x, pix_y)
    prefix = jnp.dot(lower_tri, log_trans, precision=precise, preferred_element_type=jnp.float32)
    weights = alphas * jnp.exp(prefix)
    colour = jnp.dot(params[6:9], weights, precision=precise, preferred_element_type=jnp.float32)
    totals = jnp.sum(log_trans, axis=0)
    return jnp.concatenate([colour, totals[None, :]], axis=0)


def gradient_rows(params, pix_x, pix_y, weighted, weights, weight_cot):
    features = jnp.stack(
        [jnp.ones_like(pix_x), pix_x, pix_y, pix_x * pix_x, pix_x * pix_y, pix_y * pix_y]
    )
    moments = lax.dot_general(
        features,
        weighted,
        (((1,), (1,)), ((), ())),
        precision=precise,
        preferred_element_type=jnp.float32,
    )
    colour_grad = lax.dot_general(
        weight_cot,
        weights,
        (((1,), (1,)), ((), ())),
        precision=precise,
        preferred_element_type=jnp.float32,
    )
    mean_x, mean_y, conic_a, conic_b, conic_c, opacity = (
        params[0],
        params[1],
        params[2],
        params[3],
        params[4],
        params[5],
    )
    moment_zero = moments[0]
    along_x = moments[1] - mean_x * moment_zero
    along_y = moments[2] - mean_y * moment_zero
    square_x = moments[3] - 2.0 * mean_x * moments[1] + mean_x * mean_x * moment_zero
    cross_xy = (
        moments[4] - mean_x * moments[2] - mean_y * moments[1] + mean_x * mean_y * moment_zero
    )
    square_y = moments[5] - 2.0 * mean_y * moments[2] + mean_y * mean_y * moment_zero
    grad_rows = jnp.stack(
        [
            conic_a * along_x + conic_b * along_y,
            conic_b * along_x + conic_c * along_y,
            -0.5 * square_x,
            -cross_xy,
            -0.5 * square_y,
            moment_zero / opacity,
        ]
    )
    return jnp.concatenate([grad_rows, colour_grad], axis=0)


def backward_task(params, cotangent, pix_x, pix_y, lower_tri, upper_tri):
    alphas, log_trans = splat(params, pix_x, pix_y)
    transmit = jnp.exp(
        jnp.dot(lower_tri, log_trans, precision=precise, preferred_element_type=jnp.float32)
    )
    weights = alphas * transmit
    weight_cot = cotangent[:3]
    shaded = lax.dot_general(
        params[6:9],
        weight_cot,
        (((0,), (0,)), ((), ())),
        precision=precise,
        preferred_element_type=jnp.float32,
    )
    later_sum = jnp.dot(
        upper_tri, weights * shaded, precision=precise, preferred_element_type=jnp.float32
    )
    dalpha = transmit * shaded - (later_sum + cotangent[3][None, :]) / (1.0 - alphas)
    return gradient_rows(params, pix_x, pix_y, dalpha * alphas, weights, weight_cot)


def composite(partials, live_mask, target_tile, valid_slot):
    slot_total = partials.shape[0]
    running = jnp.zeros(partials.shape[2:], jnp.float32)
    transmit = []
    for slot_index in range(slot_total):
        transmit.append(jnp.exp(running))
        running = running + partials[slot_index, 3]
    transmit = jnp.stack(transmit)
    shaded = transmit[:, None, :] * partials[:, :3]
    rendered = jnp.sum(shaded, axis=0) * live_mask
    residual = (rendered - target_tile) * live_mask
    behind = []
    running_sum = jnp.zeros_like(rendered)
    for slot_index in range(slot_total - 1, -1, -1):
        behind.insert(0, running_sum)
        running_sum = running_sum + shaded[slot_index]
    behind = jnp.stack(behind)
    valid_weight = valid_slot.astype(jnp.float32)
    weight_cot = transmit[:, None, :] * residual[None] * valid_weight[:, None, None]
    after_cot = jnp.sum(residual[None] * behind, axis=1) * valid_weight[:, None]
    return (rendered, jnp.concatenate([weight_cot, after_cot[:, None, :]], axis=1))


def shards(gaussians, seg_count, seg_block, ray_count, camera_shift, target):
    cell_count = lax.axis_size("cell")
    cell_index = lax.axis_index("cell")
    per_block = gaussians.shape[0]
    pixels = target.shape[3]
    lower_tri, upper_tri = triangles(gaussians.shape[2])
    blocks = seg_block[0, 0]
    slot_count = blocks.shape[0]
    own_count = seg_count[0, 0]
    home_cell = blocks // per_block
    local_block = blocks % per_block
    offset = (home_cell - cell_index + REACH) % cell_count - REACH
    pix_x, pix_y = pixel_frame(camera_shift[0], pixels)
    valid_slot = jnp.arange(slot_count) < own_count

    def run_forward(params):
        return forward_task(params, pix_x, pix_y, lower_tri)

    def run_backward(bundle):
        return backward_task(bundle[0], bundle[1], pix_x, pix_y, lower_tri, upper_tri)

    near_list = []
    for shift_by in range(-REACH, REACH + 1):
        if shift_by == 0:
            near_list.append(gaussians)
        else:
            near_list.append(shifted(gaussians, "cell", -shift_by))
    near_stack = jnp.concatenate(near_list, axis=0)
    pick_index = (offset + REACH) * per_block + local_block
    own_params = jnp.take(near_stack, pick_index, axis=0)
    partials = lax.map(run_forward, own_params)
    partials = jnp.where(valid_slot[:, None, None], partials, 0.0)
    live_mask = (jnp.arange(pixels) < ray_count[0, 0]).astype(jnp.float32)
    rendered, cotangent = composite(partials, live_mask, target[0, 0], valid_slot)
    own_grads = lax.map(run_backward, (own_params, cotangent))
    spot_count = (2 * REACH + 1) * per_block
    onehot = (pick_index[:, None] == jnp.arange(spot_count)[None, :]).astype(jnp.float32)
    spread = jnp.einsum("sk,sjg->kjg", onehot, own_grads, precision=precise)
    spread = spread.reshape((2 * REACH + 1, per_block) + gaussians.shape[1:])
    block_grads = spread[REACH]
    for shift_by in range(-REACH, REACH + 1):
        if shift_by != 0:
            block_grads = block_grads + shifted(spread[shift_by + REACH], "cell", shift_by)
    gauss_grad = lax.psum(block_grads, "view")
    return (rendered[None, None], gauss_grad)


def solution(mesh):
    placed = (
        P("cell", None, None),
        P("view", "cell"),
        P("view", "cell", None),
        P("view", "cell"),
        P("view", None),
        P("view", "cell", None, None),
    )
    return jax.shard_map(
        shards,
        mesh=mesh,
        in_specs=placed,
        out_specs=(P("view", "cell", None, None), P("cell", None, None)),
        check_vma=False,
    )
```

profile of v0, /device:TPU:8, one launch (start us, length us, event | category | flops | bytes accessed | tf_op | source)
XLA Modules:
  0.0 183.9 jit_solution(16609155894614825310)
XLA Ops:
  8.2 2.0 %collective-permute-start = (f32[16,9,256]{2,1,0:T(8,128)S(1)}, f32[16,9,256]{2,1,0:T(8,128)S(1)}, u32[]{:S(2)}, u32[]{:S(2)}) collective-permute-start(f32[16,9,256]{2,1,0:T(8,128)S(1)} %copy.22), channel_id=1, source_target_pairs={{248,0},{252,4},{0,8},{4,12},{8,16},{12,20},{16,24},{20,28},{24,32... | collective-permute-start | bytes 442376 | tf_op jit(solution)/shard_map/ppermute | solution.py:14
  10.2 3.9 %collective-permute-start.2 = (f32[16,9,256]{2,1,0:T(8,128)S(1)}, f32[16,9,256]{2,1,0:T(8,128)S(1)}, u32[]{:S(2)}, u32[]{:S(2)}) collective-permute-start(f32[16,9,256]{2,1,0:T(8,128)S(1)} %copy.22), channel_id=1, source_target_pairs={{4,0},{8,4},{12,8},{16,12},{20,16},{24,20},{28,24},{32,28},{36,32}... | collective-permute-start | bytes 442376 | tf_op jit(solution)/shard_map/ppermute | solution.py:14
  14.1 1.8 collective-permute-start.3
  17.2 1.4 fusion.131
  20.1 1.1 collective-permute-done
  21.9 1.2 collective-permute-done.1
  23.9 1.7 copy_dynamic-update-slice_fusion
  27.0 1.9 %gather_fusion = f32[3,9,256]{2,1,0:T(8,128)S(1)} fusion(f32[80,9,256]{2,1,0:T(8,128)} %constant_dynamic-update-slice_fusion, s32[1024]{0:T(1024)S(1)} %pad_clamp_fusion), kind=kCustom, calls=%fused_computation | custom fusion | bytes 55308 | tf_op jit(solution)/shard_map/jit(_take)/gather | solution.py:172
  29.0 30.8 %while.26 = (s32[]{:T(128)}, f32[3,4,2304]{2,1,0:T(4,128)S(1)}, f32[3,9,256]{2,1,0:T(8,128)S(1)}, f32[]{:T(128)}, f32[]{:T(128)}) while((s32[]{:T(128)}, f32[3,4,2304]{2,1,0:T(4,128)S(1)}, f32[3,9,256]{2,1,0:T(8,128)S(1)}, f32[]{:T(128)}, f32[]{:T(128)}) %tuple.102), condition=%wide.region_2.3_spmd.clone.clone, body=%wide.region_0.2_spmd.clone.sunk.clone | while | flops 1856945664 | bytes 4940977 | solution.py:173
  29.0 1.2 fusion.185
  30.2 4.6 %fusion.187 = f32[256,2304]{0,1:T(8,128)S(1)} fusion(f32[256]{0:T(256)S(1)} %bitcast.284, f32[256]{0:T(256)S(1)} %bitcast.276, f32[2304]{0:T(1024)S(1)} %get-tuple-element.382, f32[256]{0:T(256)S(1)} %bitcast.278, f32[256]{0:T(256)S(1)} %bitcast.280, f32[2304]{0:T(1024)S(1)} %get-tuple-element.385, f32[256]{0:T(256)S(1)} %bitcast.282, ...), kind=kOutput, calls=%fused_computation.19.clone.1.clone | convolution fusion | flops 1827405824 | bytes 2383872 | tf_op jit(solution)/shard_map/while/body/eval_jaxpr/dot_general | solution.py:45
  34.9 2.0 %fusion.188 = f32[3,2304]{1,0:T(4,128)S(1)} fusion(f32[256,2304]{0,1:T(8,128)S(1)} %fusion.187, f32[3,9,256]{2,1,0:T(8,128)S(1)} %get-tuple-element.451, s32[]{:T(128)} %get-tuple-element.444, s32[]{:T(128)S(6)} %add.582), kind=kOutput, calls=%fused_computation.48.clone.1.clone | convolution fusion | flops 21233664 | bytes 2391048 | tf_op jit(solution)/shard_map/while/body/eval_jaxpr/dot_general | solution.py:47
  36.9 2.3 %fusion.186 = f32[2304]{0:T(1024)S(1)} fusion(f32[256]{0:T(256)S(1)} %bitcast.285, f32[256]{0:T(256)S(1)} %bitcast.277, f32[2304]{0:T(1024)S(1)} %get-tuple-element.382, f32[256]{0:T(256)S(1)} %bitcast.279, f32[256]{0:T(256)S(1)} %bitcast.281, f32[2304]{0:T(1024)S(1)} %get-tuple-element.385, f32[256]{0:T(256)S(1)} %bitcast.283, f32[256]{0:T(256)S(1)} %bitcast.275), kind=kLoop, calls=%fused_computation.26.clone.1.clone | loop fusion | flops 8255232 | bytes 33792 | tf_op jit(solution)/shard_map/while/body/eval_jaxpr/reduce_sum | solution.py:48
  39.3 1.2 fusion.185
  40.5 4.6 %fusion.187 = f32[256,2304]{0,1:T(8,128)S(1)} fusion(f32[256]{0:T(256)S(1)} %bitcast.284, f32[256]{0:T(256)S(1)} %bitcast.276, f32[2304]{0:T(1024)S(1)} %get-tuple-element.382, f32[256]{0:T(256)S(1)} %bitcast.278, f32[256]{0:T(256)S(1)} %bitcast.280, f32[2304]{0:T(1024)S(1)} %get-tuple-element.385, f32[256]{0:T(256)S(1)} %bitcast.282, ...), kind=kOutput, calls=%fused_computation.19.clone.1.clone | convolution fusion | flops 1827405824 | bytes 2383872 | tf_op jit(solution)/shard_map/while/body/eval_jaxpr/dot_general | solution.py:45
  45.1 2.0 %fusion.188 = f32[3,2304]{1,0:T(4,128)S(1)} fusion(f32[256,2304]{0,1:T(8,128)S(1)} %fusion.187, f32[3,9,256]{2,1,0:T(8,128)S(1)} %get-tuple-element.451, s32[]{:T(128)} %get-tuple-element.444, s32[]{:T(128)S(6)} %add.582), kind=kOutput, calls=%fused_computation.48.clone.1.clone | convolution fusion | flops 21233664 | bytes 2391048 | tf_op jit(solution)/shard_map/while/body/eval_jaxpr/dot_general | solution.py:47
  47.1 2.3 %fusion.186 = f32[2304]{0:T(1024)S(1)} fusion(f32[256]{0:T(256)S(1)} %bitcast.285, f32[256]{0:T(256)S(1)} %bitcast.277, f32[2304]{0:T(1024)S(1)} %get-tuple-element.382, f32[256]{0:T(256)S(1)} %bitcast.279, f32[256]{0:T(256)S(1)} %bitcast.281, f32[2304]{0:T(1024)S(1)} %get-tuple-element.385, f32[256]{0:T(256)S(1)} %bitcast.283, f32[256]{0:T(256)S(1)} %bitcast.275), kind=kLoop, calls=%fused_computation.26.clone.1.clone | loop fusion | flops 8255232 | bytes 33792 | tf_op jit(solution)/shard_map/while/body/eval_jaxpr/reduce_sum | solution.py:48
  49.5 1.2 fusion.185
  50.8 4.6 %fusion.187 = f32[256,2304]{0,1:T(8,128)S(1)} fusion(f32[256]{0:T(256)S(1)} %bitcast.284, f32[256]{0:T(256)S(1)} %bitcast.276, f32[2304]{0:T(1024)S(1)} %get-tuple-element.382, f32[256]{0:T(256)S(1)} %bitcast.278, f32[256]{0:T(256)S(1)} %bitcast.280, f32[2304]{0:T(1024)S(1)} %get-tuple-element.385, f32[256]{0:T(256)S(1)} %bitcast.282, ...), kind=kOutput, calls=%fused_computation.19.clone.1.clone | convolution fusion | flops 1827405824 | bytes 2383872 | tf_op jit(solution)/shard_map/while/body/eval_jaxpr/dot_general | solution.py:45
  55.4 2.0 %fusion.188 = f32[3,2304]{1,0:T(4,128)S(1)} fusion(f32[256,2304]{0,1:T(8,128)S(1)} %fusion.187, f32[3,9,256]{2,1,0:T(8,128)S(1)} %get-tuple-element.451, s32[]{:T(128)} %get-tuple-element.444, s32[]{:T(128)S(6)} %add.582), kind=kOutput, calls=%fused_computation.48.clone.1.clone | convolution fusion | flops 21233664 | bytes 2391048 | tf_op jit(solution)/shard_map/while/body/eval_jaxpr/dot_general | solution.py:47
  57.4 2.3 %fusion.186 = f32[2304]{0:T(1024)S(1)} fusion(f32[256]{0:T(256)S(1)} %bitcast.285, f32[256]{0:T(256)S(1)} %bitcast.277, f32[2304]{0:T(1024)S(1)} %get-tuple-element.382, f32[256]{0:T(256)S(1)} %bitcast.279, f32[256]{0:T(256)S(1)} %bitcast.281, f32[2304]{0:T(1024)S(1)} %get-tuple-element.385, f32[256]{0:T(256)S(1)} %bitcast.283, f32[256]{0:T(256)S(1)} %bitcast.275), kind=kLoop, calls=%fused_computation.26.clone.1.clone | loop fusion | flops 8255232 | bytes 33792 | tf_op jit(solution)/shard_map/while/body/eval_jaxpr/reduce_sum | solution.py:48
  60.4 57.0 %while.27 = (s32[]{:T(128)}, f32[3,9,256]{2,0,1:T(4,128)S(1)}, f32[3,9,256]{2,1,0:T(8,128)S(1)}, f32[3,4,2304]{2,1,0:T(4,128)S(1)}, f32[]{:T(128)}, /*index=5*/f32[]{:T(128)}) while((s32[]{:T(128)}, f32[3,9,256]{2,0,1:T(4,128)S(1)}, f32[3,9,256]{2,1,0:T(8,128)S(1)}, f32[3,4,2304]{2,1,0:T(4,128)S(1)}, ...), condition=%wide.region_6.7_spmd.clone.clone.clone, body=%wide.region_5.6_spmd.clone.clone.sunk.clone | while | flops 3743404544 | bytes 35934480 | solution.py:177
  60.6 1.2 fusion.197
  61.8 4.9 %fusion.201 = f32[256,2304]{0,1:T(8,128)} fusion(f32[256]{0:T(256)S(1)} %bitcast.265, f32[256]{0:T(256)S(1)} %bitcast.256, f32[2304]{0:T(1024)S(1)} %get-tuple-element.410, f32[256]{0:T(256)S(1)} %bitcast.271, f32[256]{0:T(256)S(1)} %bitcast.259, f32[2304]{0:T(1024)S(1)} %get-tuple-element.409, f32[256]{0:T(256)S(1)} %bitcast.268, ...), kind=kOutput, calls=%fused_computation.66.clone.1.clone | convolution fusion | flops 1819738112 | bytes 2383872 | tf_op jit(solution)/shard_map/while/body/eval_jaxpr/dot_general | solution.py:102
  66.8 2.1 %fusion.200 = f32[256,2304]{0,1:T(8,128)S(1)} fusion(f32[3,4,2304]{2,1,0:T(4,128)S(1)} %get-tuple-element.469, s32[]{:T(128)} %get-tuple-element.460, f32[3,9,256]{2,1,0:T(8,128)S(1)} %get-tuple-element.468, s32[]{:T(128)S(6)} %add.601), kind=kOutput, calls=%fused_computation.88.clone.1.clone | convolution fusion | flops 21233664 | bytes 2401284 | tf_op jit(solution)/shard_map/while/body/eval_jaxpr/dot_general | solution.py:106
  68.9 4.4 %fusion.202 = f32[256,2304]{0,1:T(8,128)S(1)} fusion(f32[256,2304]{0,1:T(8,128)S(1)} %fusion.200, f32[256,2304]{0,1:T(8,128)S(1)} %copy-done.1, f32[2304]{0:T(1024)S(1)} %dynamic-slice_reduce_fusion.3, f32[256]{0:T(256)S(1)} %bitcast.266, f32[256]{0:T(256)S(1)} %bitcast.257, f32[2304]{0:T(1024)S(1)} %get-tuple-element.410, ...), kind=kOutput, calls=%fused_computation.70.clone.1.clone | convolution fusion | flops 1830944768 | bytes 7111680 | tf_op jit(solution)/shard_map/while/body/eval_jaxpr/dot_general | solution.py:113
  73.4 1.2 fusion.199
  75.4 1.0 fusion.203
  77.0 2.2 %fusion.205 = f32[3,256]{1,0:T(4,128)S(1)} fusion(f32[256,2304]{0,1:T(8,128)S(1)} %copy-done.2, f32[256]{0:T(256)S(1)} %bitcast.267, f32[256]{0:T(256)S(1)} %bitcast.258, f32[2304]{0:T(1024)S(1)} %get-tuple-element.410, f32[256]{0:T(256)S(1)} %bitcast.273, f32[256]{0:T(256)S(1)} %bitcast.261, f32[2304]{0:T(1024)S(1)} %get-tuple-element.409, ...), kind=kOutput, calls=%fused_computation.80.clone.1.clone | convolution fusion | flops 28901376 | bytes 2429956 | tf_op jit(solution)/shard_map/while/body/eval_jaxpr/dot_general | solution.py:63
  79.5 1.2 fusion.197
  80.7 4.9 %fusion.201 = f32[256,2304]{0,1:T(8,128)} fusion(f32[256]{0:T(256)S(1)} %bitcast.265, f32[256]{0:T(256)S(1)} %bitcast.256, f32[2304]{0:T(1024)S(1)} %get-tuple-element.410, f32[256]{0:T(256)S(1)} %bitcast.271, f32[256]{0:T(256)S(1)} %bitcast.259, f32[2304]{0:T(1024)S(1)} %get-tuple-element.409, f32[256]{0:T(256)S(1)} %bitcast.268, ...), kind=kOutput, calls=%fused_computation.66.clone.1.clone | convolution fusion | flops 1819738112 | bytes 2383872 | tf_op jit(solution)/shard_map/while/body/eval_jaxpr/dot_general | solution.py:102
  85.6 2.1 %fusion.200 = f32[256,2304]{0,1:T(8,128)S(1)} fusion(f32[3,4,2304]{2,1,0:T(4,128)S(1)} %get-tuple-element.469, s32[]{:T(128)} %get-tuple-element.460, f32[3,9,256]{2,1,0:T(8,128)S(1)} %get-tuple-element.468, s32[]{:T(128)S(6)} %add.601), kind=kOutput, calls=%fused_computation.88.clone.1.clone | convolution fusion | flops 21233664 | bytes 2401284 | tf_op jit(solution)/shard_map/while/body/eval_jaxpr/dot_general | solution.py:106
  87.8 4.4 %fusion.202 = f32[256,2304]{0,1:T(8,128)S(1)} fusion(f32[256,2304]{0,1:T(8,128)S(1)} %fusion.200, f32[256,2304]{0,1:T(8,128)S(1)} %copy-done.1, f32[2304]{0:T(1024)S(1)} %dynamic-slice_reduce_fusion.3, f32[256]{0:T(256)S(1)} %bitcast.266, f32[256]{0:T(256)S(1)} %bitcast.257, f32[2304]{0:T(1024)S(1)} %get-tuple-element.410, ...), kind=kOutput, calls=%fused_computation.70.clone.1.clone | convolution fusion | flops 1830944768 | bytes 7111680 | tf_op jit(solution)/shard_map/while/body/eval_jaxpr/dot_general | solution.py:113
  92.2 1.2 fusion.199
  94.2 1.0 fusion.203
  95.9 2.2 %fusion.205 = f32[3,256]{1,0:T(4,128)S(1)} fusion(f32[256,2304]{0,1:T(8,128)S(1)} %copy-done.2, f32[256]{0:T(256)S(1)} %bitcast.267, f32[256]{0:T(256)S(1)} %bitcast.258, f32[2304]{0:T(1024)S(1)} %get-tuple-element.410, f32[256]{0:T(256)S(1)} %bitcast.273, f32[256]{0:T(256)S(1)} %bitcast.261, f32[2304]{0:T(1024)S(1)} %get-tuple-element.409, ...), kind=kOutput, calls=%fused_computation.80.clone.1.clone | convolution fusion | flops 28901376 | bytes 2429956 | tf_op jit(solution)/shard_map/while/body/eval_jaxpr/dot_general | solution.py:63
  98.4 1.2 fusion.197
  99.6 4.9 %fusion.201 = f32[256,2304]{0,1:T(8,128)} fusion(f32[256]{0:T(256)S(1)} %bitcast.265, f32[256]{0:T(256)S(1)} %bitcast.256, f32[2304]{0:T(1024)S(1)} %get-tuple-element.410, f32[256]{0:T(256)S(1)} %bitcast.271, f32[256]{0:T(256)S(1)} %bitcast.259, f32[2304]{0:T(1024)S(1)} %get-tuple-element.409, f32[256]{0:T(256)S(1)} %bitcast.268, ...), kind=kOutput, calls=%fused_computation.66.clone.1.clone | convolution fusion | flops 1819738112 | bytes 2383872 | tf_op jit(solution)/shard_map/while/body/eval_jaxpr/dot_general | solution.py:102
  104.5 2.1 %fusion.200 = f32[256,2304]{0,1:T(8,128)S(1)} fusion(f32[3,4,2304]{2,1,0:T(4,128)S(1)} %get-tuple-element.469, s32[]{:T(128)} %get-tuple-element.460, f32[3,9,256]{2,1,0:T(8,128)S(1)} %get-tuple-element.468, s32[]{:T(128)S(6)} %add.601), kind=kOutput, calls=%fused_computation.88.clone.1.clone | convolution fusion | flops 21233664 | bytes 2401284 | tf_op jit(solution)/shard_map/while/body/eval_jaxpr/dot_general | solution.py:106
  106.7 4.4 %fusion.202 = f32[256,2304]{0,1:T(8,128)S(1)} fusion(f32[256,2304]{0,1:T(8,128)S(1)} %fusion.200, f32[256,2304]{0,1:T(8,128)S(1)} %copy-done.1, f32[2304]{0:T(1024)S(1)} %dynamic-slice_reduce_fusion.3, f32[256]{0:T(256)S(1)} %bitcast.266, f32[256]{0:T(256)S(1)} %bitcast.257, f32[2304]{0:T(1024)S(1)} %get-tuple-element.410, ...), kind=kOutput, calls=%fused_computation.70.clone.1.clone | convolution fusion | flops 1830944768 | bytes 7111680 | tf_op jit(solution)/shard_map/while/body/eval_jaxpr/dot_general | solution.py:113
  111.1 1.2 fusion.199
  114.7 2.2 %fusion.205 = f32[3,256]{1,0:T(4,128)S(1)} fusion(f32[256,2304]{0,1:T(8,128)S(1)} %copy-done.2, f32[256]{0:T(256)S(1)} %bitcast.267, f32[256]{0:T(256)S(1)} %bitcast.258, f32[2304]{0:T(1024)S(1)} %get-tuple-element.410, f32[256]{0:T(256)S(1)} %bitcast.273, f32[256]{0:T(256)S(1)} %bitcast.261, f32[2304]{0:T(1024)S(1)} %get-tuple-element.409, ...), kind=kOutput, calls=%fused_computation.80.clone.1.clone | convolution fusion | flops 28901376 | bytes 2429956 | tf_op jit(solution)/shard_map/while/body/eval_jaxpr/dot_general | solution.py:63
  118.0 1.8 collective-permute-start.4
  120.6 2.6 %collective-permute-done.4 = f32[16,9,256]{2,0,1:T(8,128)S(1)} collective-permute-done((f32[16,9,256]{2,0,1:T(8,128)S(1)}, f32[16,9,256]{2,0,1:T(8,128)S(1)}, u32[]{:S(2)}, u32[]{:S(2)}) %collective-permute-start.4) | collective-permute-done | bytes 147488 | tf_op jit(solution)/shard_map/ppermute | solution.py:14
  124.1 2.9 %collective-permute-done.6 = f32[16,9,256]{2,0,1:T(8,128)S(1)} collective-permute-done((f32[16,9,256]{2,0,1:T(8,128)S(1)}, f32[16,9,256]{2,0,1:T(8,128)S(1)}, u32[]{:S(2)}, u32[]{:S(2)}) %collective-permute-start.6) | collective-permute-done | bytes 147488 | tf_op jit(solution)/shard_map/ppermute | solution.py:14
  127.0 2.2 %collective-permute-done.7 = f32[16,9,256]{2,0,1:T(8,128)S(1)} collective-permute-done((f32[16,9,256]{2,0,1:T(8,128)S(1)}, f32[16,9,256]{2,0,1:T(8,128)S(1)}, u32[]{:S(2)}, u32[]{:S(2)}) %collective-permute-start.7) | collective-permute-done | bytes 147488 | tf_op jit(solution)/shard_map/ppermute | solution.py:14
  130.5 44.9 %all-reduce.2.cloned.1.call-done = f32[16,9,256]{2,0,1:T(8,128)} async-done(((f32[16,9,256]{2,0,1:T(8,128)}), f32[16,9,256]{2,0,1:T(8,128)}) %all-reduce.2.cloned.1.call-update) | async-done | bytes 147472 | tf_op jit(solution)/shard_map/psum | solution.py:186
  175.5 1.6 copy.63
  (97 shorter events, 15.7 us)
Async XLA Ops:
  7.2 168.3 %all-reduce.2.cloned.1.call-start = ((), (), s32[]{:S(2)}) async-start(), calls=%async_computation | async-start | bytes 294912 | tf_op jit(solution)/shard_map/psum | solution.py:186
  8.2 13.0 %collective-permute-start = (f32[16,9,256]{2,1,0:T(8,128)S(1)}, f32[16,9,256]{2,1,0:T(8,128)S(1)}, u32[]{:S(2)}, u32[]{:S(2)}) collective-permute-start(f32[16,9,256]{2,1,0:T(8,128)S(1)} %copy.22), channel_id=1, source_target_pairs={{248,0},{252,4},{0,8},{4,12},{8,16},{12,20},{16,24},{20,28},{24,32... | collective-permute-start | bytes 442376 | tf_op jit(solution)/shard_map/ppermute | solution.py:14
  10.2 12.9 %collective-permute-start.1 = (f32[16,9,256]{2,1,0:T(8,128)S(1)}, f32[16,9,256]{2,1,0:T(8,128)S(1)}, u32[]{:S(2)}, u32[]{:S(2)}) collective-permute-start(f32[16,9,256]{2,1,0:T(8,128)S(1)} %copy.22), channel_id=1, source_target_pairs={{252,0},{0,4},{4,8},{8,12},{12,16},{16,20},{20,24},{24,28},{28,32}... | collective-permute-start | bytes 442376 | tf_op jit(solution)/shard_map/ppermute | solution.py:14
  10.2 15.4 %collective-permute-start.2 = (f32[16,9,256]{2,1,0:T(8,128)S(1)}, f32[16,9,256]{2,1,0:T(8,128)S(1)}, u32[]{:S(2)}, u32[]{:S(2)}) collective-permute-start(f32[16,9,256]{2,1,0:T(8,128)S(1)} %copy.22), channel_id=1, source_target_pairs={{4,0},{8,4},{12,8},{16,12},{20,16},{24,20},{28,24},{32,28},{36,32}... | collective-permute-start | bytes 442376 | tf_op jit(solution)/shard_map/ppermute | solution.py:14
  14.1 12.2 %collective-permute-start.3 = (f32[16,9,256]{2,1,0:T(8,128)S(1)}, f32[16,9,256]{2,1,0:T(8,128)S(1)}, u32[]{:S(2)}, u32[]{:S(2)}) collective-permute-start(f32[16,9,256]{2,1,0:T(8,128)S(1)} %copy.22), channel_id=1, source_target_pairs={{8,0},{12,4},{16,8},{20,12},{24,16},{28,20},{32,24},{36,28},{40,32... | collective-permute-start | bytes 442376 | tf_op jit(solution)/shard_map/ppermute | solution.py:14
  29.0 31.1 %copy-start = (f32[1,1,3,2304]{3,1,2,0:T(1,128)S(1)}, f32[1,1,3,2304]{3,1,2,0:T(1,128)}, u32[]{:S(2)}) copy-start(f32[1,1,3,2304]{3,1,2,0:T(1,128)} %param.15) | copy-start | bytes 82948
  66.8 2.2 %copy-start.1 = (f32[256,2304]{0,1:T(8,128)S(1)}, f32[256,2304]{0,1:T(8,128)}, u32[]{:S(2)}) copy-start(f32[256,2304]{0,1:T(8,128)} %fusion.201) | copy-start | bytes 7077892 | tf_op jit(solution)/shard_map/while
  75.3 1.7 copy-start.2
  85.6 2.2 %copy-start.1 = (f32[256,2304]{0,1:T(8,128)S(1)}, f32[256,2304]{0,1:T(8,128)}, u32[]{:S(2)}) copy-start(f32[256,2304]{0,1:T(8,128)} %fusion.201) | copy-start | bytes 7077892 | tf_op jit(solution)/shard_map/while
  94.2 1.7 copy-start.2
  104.5 2.2 %copy-start.1 = (f32[256,2304]{0,1:T(8,128)S(1)}, f32[256,2304]{0,1:T(8,128)}, u32[]{:S(2)}) copy-start(f32[256,2304]{0,1:T(8,128)} %fusion.201) | copy-start | bytes 7077892 | tf_op jit(solution)/shard_map/while
  113.1 1.7 copy-start.2
  118.0 5.2 %collective-permute-start.4 = (f32[16,9,256]{2,0,1:T(8,128)S(1)}, f32[16,9,256]{2,0,1:T(8,128)S(1)}, u32[]{:S(2)}, u32[]{:S(2)}) collective-permute-start(f32[16,9,256]{2,0,1:T(8,128)S(1)} %get-tuple-element.244), channel_id=1, source_target_pairs={{8,0},{12,4},{16,8},{20,12},{24,16},{28,20},{32,24},{36,28},{40,32... | collective-permute-start | bytes 442376 | tf_op jit(solution)/shard_map/ppermute | solution.py:14
  119.8 4.2 %collective-permute-start.5 = (f32[16,9,256]{2,0,1:T(8,128)S(1)}, f32[16,9,256]{2,0,1:T(8,128)S(1)}, u32[]{:S(2)}, u32[]{:S(2)}) collective-permute-start(f32[16,9,256]{2,0,1:T(8,128)S(1)} %get-tuple-element.247), channel_id=1, source_target_pairs={{4,0},{8,4},{12,8},{16,12},{20,16},{24,20},{28,24},{32,28},{36,32}... | collective-permute-start | bytes 442376 | tf_op jit(solution)/shard_map/ppermute | solution.py:14
  119.8 7.2 %collective-permute-start.6 = (f32[16,9,256]{2,0,1:T(8,128)S(1)}, f32[16,9,256]{2,0,1:T(8,128)S(1)}, u32[]{:S(2)}, u32[]{:S(2)}) collective-permute-start(f32[16,9,256]{2,0,1:T(8,128)S(1)} %get-tuple-element.246), channel_id=1, source_target_pairs={{252,0},{0,4},{4,8},{8,12},{12,16},{16,20},{20,24},{24,28},{28,32}... | collective-permute-start | bytes 442376 | tf_op jit(solution)/shard_map/ppermute | solution.py:14
  120.3 8.8 %collective-permute-start.7 = (f32[16,9,256]{2,0,1:T(8,128)S(1)}, f32[16,9,256]{2,0,1:T(8,128)S(1)}, u32[]{:S(2)}, u32[]{:S(2)}) collective-permute-start(f32[16,9,256]{2,0,1:T(8,128)S(1)} %get-tuple-element.245), channel_id=1, source_target_pairs={{248,0},{252,4},{0,8},{4,12},{8,16},{12,20},{16,24},{20,28},{24,32... | collective-permute-start | bytes 442376 | tf_op jit(solution)/shard_map/ppermute | solution.py:14
Sparse Core Ops, SparseCore 0:
  130.0 45.3 all-reduce.1
where the time goes:
time: 184 us
  matrix products  64.5 us (35%)
  waiting for transfers between devices  55.8 us (30%)
  other arithmetic  23.4 us (13%)
  between operations  15.5 us (8%)
  local copies, waits for them, and re-layouts  13.4 us (7%)
  starting transfers between devices  10.3 us (6%)
    psum x1, waiting for transfers between devices, shards(): gauss_grad = lax.psum(block_grads, 'view')  44.9 us
    dot_general x3, matrix products, backward_task(): jnp.dot(lower_tri, log_trans, precision=precise, preferred_element_type=j...  14.8 us
    dot_general x3, matrix products, forward_task(): jnp.dot(lower_tri, log_trans, precision=precise, preferred_element_type=j...  13.9 us
    dot_general x3, matrix products, backward_task(): jnp.dot(upper_tri, weights * shaded, precision=precise, preferred_element...  13.2 us
    ppermute x8, waiting for transfers between devices, shifted(): return lax.ppermute(block, axis, route)  10.9 us
    ppermute x8, starting transfers between devices, shifted(): return lax.ppermute(block, axis, route)  10.3 us
    sub x6, other arithmetic, pixel_frame(): pix_y = (pixel_ids // TILE).astype(jnp.float32) - centre - shift[1]  7.23 us
    reduce_sum x3, other arithmetic, forward_task(): totals = jnp.sum(log_trans, axis=0)  6.89 us
  transfers between devices with their start and end apart: 9, of which 7 were waited for; matrix products, arithmetic and copies ran while one was open for 4% of the time, Pallas kernels for 0%

commit v1 on v0

--- a/solution.py
+++ b/solution.py
@@ -2,6 +2,7 @@
 import jax.numpy as jnp
 from jax import lax
 from jax.sharding import PartitionSpec as P
+from jax.lax import all_gather
 
 TILE = 48
 REACH = 2
@@ -183,7 +184,7 @@
     for shift_by in range(-REACH, REACH + 1):
         if shift_by != 0:
             block_grads = block_grads + shifted(spread[shift_by + REACH], "cell", shift_by)
-    gauss_grad = lax.psum(block_grads, "view")
+    gauss_grad = jnp.sum(all_gather(block_grads, axis_name="view"), axis=0)
     return (rendered[None, None], gauss_grad)
 
 

time: 184 us -> 143 us (0.78)
  the two profiles are of different devices: /device:TPU:8 before, /device:TPU:2 now
where the time goes in v1:
time: 143 us
  matrix products  64.5 us (45%)
  other arithmetic  24.4 us (17%)
  blocking collectives  13.9 us (10%)
  starting transfers between devices  13.5 us (9%)
  local copies, waits for them, and re-layouts  11.8 us (8%)
  waiting for transfers between devices  11.8 us (8%)
  between operations  2.08 us (1%)
    dot_general x3, matrix products, backward_task(): jnp.dot(lower_tri, log_trans, precision=precise, preferred_element_type=j...  14.8 us
    dot_general x3, matrix products, forward_task(): jnp.dot(lower_tri, log_trans, precision=precise, preferred_element_type=j...  13.9 us
    all_gather x1, blocking collectives, shards(): gauss_grad = jnp.sum(all_gather(block_grads, axis_name='view'), axis=0)  13.9 us
    ppermute x8, starting transfers between devices, shifted(): return lax.ppermute(block, axis, route)  13.5 us
    dot_general x3, matrix products, backward_task(): jnp.dot(upper_tri, weights * shaded, precision=precise, preferred_element...  13.2 us
    ppermute x8, waiting for transfers between devices, shifted(): return lax.ppermute(block, axis, route)  11.8 us
    sub x6, other arithmetic, pixel_frame(): pix_y = (pixel_ids // TILE).astype(jnp.float32) - centre - shift[1]  7.6 us
    reduce_sum x3, other arithmetic, forward_task(): totals = jnp.sum(log_trans, axis=0)  6.88 us
  transfers between devices with their start and end apart: 8, of which 6 were waited for; matrix products, arithmetic and copies ran while one was open for 5% of the time, Pallas kernels for 0%

profile of v1, /device:TPU:2, one launch (start us, length us, event | category | flops | bytes accessed | tf_op | source)
XLA Modules:
  0.0 142.8 jit_solution(11425719154649782178)
XLA Ops:
  1.6 2.0 %collective-permute-start = (f32[16,9,256]{2,1,0:T(8,128)S(1)}, f32[16,9,256]{2,1,0:T(8,128)S(1)}, u32[]{:S(2)}, u32[]{:S(2)}) collective-permute-start(f32[16,9,256]{2,1,0:T(8,128)S(1)} %copy.22), channel_id=1, source_target_pairs={{248,0},{252,4},{0,8},{4,12},{8,16},{12,20},{16,24},{20,28},{24,32... | collective-permute-start | bytes 442376 | tf_op jit(solution)/shard_map/ppermute | solution.py:15
  3.6 6.0 %collective-permute-start.2 = (f32[16,9,256]{2,1,0:T(8,128)S(1)}, f32[16,9,256]{2,1,0:T(8,128)S(1)}, u32[]{:S(2)}, u32[]{:S(2)}) collective-permute-start(f32[16,9,256]{2,1,0:T(8,128)S(1)} %copy.22), channel_id=1, source_target_pairs={{4,0},{8,4},{12,8},{16,12},{20,16},{24,20},{28,24},{32,28},{36,32}... | collective-permute-start | bytes 442376 | tf_op jit(solution)/shard_map/ppermute | solution.py:15
  9.6 2.2 %collective-permute-start.3 = (f32[16,9,256]{2,1,0:T(8,128)S(1)}, f32[16,9,256]{2,1,0:T(8,128)S(1)}, u32[]{:S(2)}, u32[]{:S(2)}) collective-permute-start(f32[16,9,256]{2,1,0:T(8,128)S(1)} %copy.22), channel_id=1, source_target_pairs={{8,0},{12,4},{16,8},{20,12},{24,16},{28,20},{32,24},{36,28},{40,32... | collective-permute-start | bytes 442376 | tf_op jit(solution)/shard_map/ppermute | solution.py:15
  13.2 1.3 fusion.131
  16.0 1.2 collective-permute-done
  17.9 1.2 collective-permute-done.1
  19.9 1.7 %copy_dynamic-update-slice_fusion = f32[80,9,256]{2,1,0:T(8,128)} fusion(f32[80,9,256]{2,1,0:T(8,128)} %constant_dynamic-update-slice_fusion.2, f32[16,9,256]{2,0,1:T(8,128)} %param.10), kind=kLoop, calls=%fused_computation.174 | loop fusion | bytes 409600
  23.0 1.9 %gather_fusion = f32[3,9,256]{2,1,0:T(8,128)S(1)} fusion(f32[80,9,256]{2,1,0:T(8,128)} %constant_dynamic-update-slice_fusion, s32[1024]{0:T(1024)S(1)} %pad_clamp_fusion), kind=kCustom, calls=%fused_computation | custom fusion | bytes 55308 | tf_op jit(solution)/shard_map/jit(_take)/gather | solution.py:173
  25.0 31.0 %while.26 = (s32[]{:T(128)}, f32[3,4,2304]{2,1,0:T(4,128)S(1)}, f32[3,9,256]{2,1,0:T(8,128)S(1)}, f32[]{:T(128)}, f32[]{:T(128)}) while((s32[]{:T(128)}, f32[3,4,2304]{2,1,0:T(4,128)S(1)}, f32[3,9,256]{2,1,0:T(8,128)S(1)}, f32[]{:T(128)}, f32[]{:T(128)}) %tuple.102), condition=%wide.region_2.3_spmd.clone.clone, body=%wide.region_0.2_spmd.clone.sunk.clone | while | flops 1856945664 | bytes 4940977 | solution.py:174
  25.0 1.3 fusion.185
  26.3 4.6 %fusion.187 = f32[256,2304]{0,1:T(8,128)S(1)} fusion(f32[256]{0:T(256)S(1)} %bitcast.286, f32[256]{0:T(256)S(1)} %bitcast.278, f32[2304]{0:T(1024)S(1)} %get-tuple-element.382, f32[256]{0:T(256)S(1)} %bitcast.280, f32[256]{0:T(256)S(1)} %bitcast.282, f32[2304]{0:T(1024)S(1)} %get-tuple-element.385, f32[256]{0:T(256)S(1)} %bitcast.284, ...), kind=kOutput, calls=%fused_computation.19.clone.1.clone | convolution fusion | flops 1827405824 | bytes 2383872 | tf_op jit(solution)/shard_map/while/body/eval_jaxpr/dot_general | solution.py:46
  30.9 2.0 %fusion.188 = f32[3,2304]{1,0:T(4,128)S(1)} fusion(f32[256,2304]{0,1:T(8,128)S(1)} %fusion.187, f32[3,9,256]{2,1,0:T(8,128)S(1)} %get-tuple-element.451, s32[]{:T(128)} %get-tuple-element.444, s32[]{:T(128)S(6)} %add.580), kind=kOutput, calls=%fused_computation.48.clone.1.clone | convolution fusion | flops 21233664 | bytes 2391048 | tf_op jit(solution)/shard_map/while/body/eval_jaxpr/dot_general | solution.py:48
  32.9 2.3 %fusion.186 = f32[2304]{0:T(1024)S(1)} fusion(f32[256]{0:T(256)S(1)} %bitcast.287, f32[256]{0:T(256)S(1)} %bitcast.279, f32[2304]{0:T(1024)S(1)} %get-tuple-element.382, f32[256]{0:T(256)S(1)} %bitcast.281, f32[256]{0:T(256)S(1)} %bitcast.283, f32[2304]{0:T(1024)S(1)} %get-tuple-element.385, f32[256]{0:T(256)S(1)} %bitcast.285, f32[256]{0:T(256)S(1)} %bitcast.277), kind=kLoop, calls=%fused_computation.26.clone.1.clone | loop fusion | flops 8255232 | bytes 33792 | tf_op jit(solution)/shard_map/while/body/eval_jaxpr/reduce_sum | solution.py:49
  35.3 1.3 fusion.185
  36.6 4.6 %fusion.187 = f32[256,2304]{0,1:T(8,128)S(1)} fusion(f32[256]{0:T(256)S(1)} %bitcast.286, f32[256]{0:T(256)S(1)} %bitcast.278, f32[2304]{0:T(1024)S(1)} %get-tuple-element.382, f32[256]{0:T(256)S(1)} %bitcast.280, f32[256]{0:T(256)S(1)} %bitcast.282, f32[2304]{0:T(1024)S(1)} %get-tuple-element.385, f32[256]{0:T(256)S(1)} %bitcast.284, ...), kind=kOutput, calls=%fused_computation.19.clone.1.clone | convolution fusion | flops 1827405824 | bytes 2383872 | tf_op jit(solution)/shard_map/while/body/eval_jaxpr/dot_general | solution.py:46
  41.2 2.0 %fusion.188 = f32[3,2304]{1,0:T(4,128)S(1)} fusion(f32[256,2304]{0,1:T(8,128)S(1)} %fusion.187, f32[3,9,256]{2,1,0:T(8,128)S(1)} %get-tuple-element.451, s32[]{:T(128)} %get-tuple-element.444, s32[]{:T(128)S(6)} %add.580), kind=kOutput, calls=%fused_computation.48.clone.1.clone | convolution fusion | flops 21233664 | bytes 2391048 | tf_op jit(solution)/shard_map/while/body/eval_jaxpr/dot_general | solution.py:48
  43.3 2.3 %fusion.186 = f32[2304]{0:T(1024)S(1)} fusion(f32[256]{0:T(256)S(1)} %bitcast.287, f32[256]{0:T(256)S(1)} %bitcast.279, f32[2304]{0:T(1024)S(1)} %get-tuple-element.382, f32[256]{0:T(256)S(1)} %bitcast.281, f32[256]{0:T(256)S(1)} %bitcast.283, f32[2304]{0:T(1024)S(1)} %get-tuple-element.385, f32[256]{0:T(256)S(1)} %bitcast.285, f32[256]{0:T(256)S(1)} %bitcast.277), kind=kLoop, calls=%fused_computation.26.clone.1.clone | loop fusion | flops 8255232 | bytes 33792 | tf_op jit(solution)/shard_map/while/body/eval_jaxpr/reduce_sum | solution.py:49
  45.7 1.3 fusion.185
  46.9 4.6 %fusion.187 = f32[256,2304]{0,1:T(8,128)S(1)} fusion(f32[256]{0:T(256)S(1)} %bitcast.286, f32[256]{0:T(256)S(1)} %bitcast.278, f32[2304]{0:T(1024)S(1)} %get-tuple-element.382, f32[256]{0:T(256)S(1)} %bitcast.280, f32[256]{0:T(256)S(1)} %bitcast.282, f32[2304]{0:T(1024)S(1)} %get-tuple-element.385, f32[256]{0:T(256)S(1)} %bitcast.284, ...), kind=kOutput, calls=%fused_computation.19.clone.1.clone | convolution fusion | flops 1827405824 | bytes 2383872 | tf_op jit(solution)/shard_map/while/body/eval_jaxpr/dot_general | solution.py:46
  51.6 2.0 %fusion.188 = f32[3,2304]{1,0:T(4,128)S(1)} fusion(f32[256,2304]{0,1:T(8,128)S(1)} %fusion.187, f32[3,9,256]{2,1,0:T(8,128)S(1)} %get-tuple-element.451, s32[]{:T(128)} %get-tuple-element.444, s32[]{:T(128)S(6)} %add.580), kind=kOutput, calls=%fused_computation.48.clone.1.clone | convolution fusion | flops 21233664 | bytes 2391048 | tf_op jit(solution)/shard_map/while/body/eval_jaxpr/dot_general | solution.py:48
  53.6 2.3 %fusion.186 = f32[2304]{0:T(1024)S(1)} fusion(f32[256]{0:T(256)S(1)} %bitcast.287, f32[256]{0:T(256)S(1)} %bitcast.279, f32[2304]{0:T(1024)S(1)} %get-tuple-element.382, f32[256]{0:T(256)S(1)} %bitcast.281, f32[256]{0:T(256)S(1)} %bitcast.283, f32[2304]{0:T(1024)S(1)} %get-tuple-element.385, f32[256]{0:T(256)S(1)} %bitcast.285, f32[256]{0:T(256)S(1)} %bitcast.277), kind=kLoop, calls=%fused_computation.26.clone.1.clone | loop fusion | flops 8255232 | bytes 33792 | tf_op jit(solution)/shard_map/while/body/eval_jaxpr/reduce_sum | solution.py:49
  56.6 57.7 %while.27 = (s32[]{:T(128)}, f32[3,9,256]{2,0,1:T(4,128)S(1)}, f32[3,9,256]{2,1,0:T(8,128)S(1)}, f32[3,4,2304]{2,1,0:T(4,128)S(1)}, f32[]{:T(128)}, /*index=5*/f32[]{:T(128)}) while((s32[]{:T(128)}, f32[3,9,256]{2,0,1:T(4,128)S(1)}, f32[3,9,256]{2,1,0:T(8,128)S(1)}, f32[3,4,2304]{2,1,0:T(4,128)S(1)}, ...), condition=%wide.region_6.7_spmd.clone.clone.clone, body=%wide.region_5.6_spmd.clone.clone.sunk.clone | while | flops 3743404544 | bytes 35934480 | solution.py:178
  56.8 1.3 fusion.197
  58.1 4.9 %fusion.201 = f32[256,2304]{0,1:T(8,128)} fusion(f32[256]{0:T(256)S(1)} %bitcast.267, f32[256]{0:T(256)S(1)} %bitcast.258, f32[2304]{0:T(1024)S(1)} %get-tuple-element.410, f32[256]{0:T(256)S(1)} %bitcast.273, f32[256]{0:T(256)S(1)} %bitcast.261, f32[2304]{0:T(1024)S(1)} %get-tuple-element.409, f32[256]{0:T(256)S(1)} %bitcast.270, ...), kind=kOutput, calls=%fused_computation.66.clone.1.clone | convolution fusion | flops 1819738112 | bytes 2383872 | tf_op jit(solution)/shard_map/while/body/eval_jaxpr/dot_general | solution.py:103
  63.0 2.1 %fusion.200 = f32[256,2304]{0,1:T(8,128)S(1)} fusion(f32[3,4,2304]{2,1,0:T(4,128)S(1)} %get-tuple-element.469, s32[]{:T(128)} %get-tuple-element.460, f32[3,9,256]{2,1,0:T(8,128)S(1)} %get-tuple-element.468, s32[]{:T(128)S(6)} %add.599), kind=kOutput, calls=%fused_computation.88.clone.1.clone | convolution fusion | flops 21233664 | bytes 2401284 | tf_op jit(solution)/shard_map/while/body/eval_jaxpr/dot_general | solution.py:107
  65.2 4.4 %fusion.202 = f32[256,2304]{0,1:T(8,128)S(1)} fusion(f32[256,2304]{0,1:T(8,128)S(1)} %fusion.200, f32[256,2304]{0,1:T(8,128)S(1)} %copy-done.1, f32[2304]{0:T(1024)S(1)} %dynamic-slice_reduce_fusion.3, f32[256]{0:T(256)S(1)} %bitcast.268, f32[256]{0:T(256)S(1)} %bitcast.259, f32[2304]{0:T(1024)S(1)} %get-tuple-element.410, ...), kind=kOutput, calls=%fused_computation.70.clone.1.clone | convolution fusion | flops 1830944768 | bytes 7111680 | tf_op jit(solution)/shard_map/while/body/eval_jaxpr/dot_general | solution.py:114
  69.6 1.3 fusion.199
  71.8 1.0 fusion.203
  73.4 2.2 %fusion.205 = f32[3,256]{1,0:T(4,128)S(1)} fusion(f32[256,2304]{0,1:T(8,128)S(1)} %copy-done.2, f32[256]{0:T(256)S(1)} %bitcast.269, f32[256]{0:T(256)S(1)} %bitcast.260, f32[2304]{0:T(1024)S(1)} %get-tuple-element.410, f32[256]{0:T(256)S(1)} %bitcast.275, f32[256]{0:T(256)S(1)} %bitcast.263, f32[2304]{0:T(1024)S(1)} %get-tuple-element.409, ...), kind=kOutput, calls=%fused_computation.80.clone.1.clone | convolution fusion | flops 28901376 | bytes 2429956 | tf_op jit(solution)/shard_map/while/body/eval_jaxpr/dot_general | solution.py:64
  75.9 1.3 fusion.197
  77.2 4.9 %fusion.201 = f32[256,2304]{0,1:T(8,128)} fusion(f32[256]{0:T(256)S(1)} %bitcast.267, f32[256]{0:T(256)S(1)} %bitcast.258, f32[2304]{0:T(1024)S(1)} %get-tuple-element.410, f32[256]{0:T(256)S(1)} %bitcast.273, f32[256]{0:T(256)S(1)} %bitcast.261, f32[2304]{0:T(1024)S(1)} %get-tuple-element.409, f32[256]{0:T(256)S(1)} %bitcast.270, ...), kind=kOutput, calls=%fused_computation.66.clone.1.clone | convolution fusion | flops 1819738112 | bytes 2383872 | tf_op jit(solution)/shard_map/while/body/eval_jaxpr/dot_general | solution.py:103
  82.1 2.1 %fusion.200 = f32[256,2304]{0,1:T(8,128)S(1)} fusion(f32[3,4,2304]{2,1,0:T(4,128)S(1)} %get-tuple-element.469, s32[]{:T(128)} %get-tuple-element.460, f32[3,9,256]{2,1,0:T(8,128)S(1)} %get-tuple-element.468, s32[]{:T(128)S(6)} %add.599), kind=kOutput, calls=%fused_computation.88.clone.1.clone | convolution fusion | flops 21233664 | bytes 2401284 | tf_op jit(solution)/shard_map/while/body/eval_jaxpr/dot_general | solution.py:107
  84.3 4.4 %fusion.202 = f32[256,2304]{0,1:T(8,128)S(1)} fusion(f32[256,2304]{0,1:T(8,128)S(1)} %fusion.200, f32[256,2304]{0,1:T(8,128)S(1)} %copy-done.1, f32[2304]{0:T(1024)S(1)} %dynamic-slice_reduce_fusion.3, f32[256]{0:T(256)S(1)} %bitcast.268, f32[256]{0:T(256)S(1)} %bitcast.259, f32[2304]{0:T(1024)S(1)} %get-tuple-element.410, ...), kind=kOutput, calls=%fused_computation.70.clone.1.clone | convolution fusion | flops 1830944768 | bytes 7111680 | tf_op jit(solution)/shard_map/while/body/eval_jaxpr/dot_general | solution.py:114
  88.7 1.3 fusion.199
  90.9 1.0 fusion.203
  92.5 2.2 %fusion.205 = f32[3,256]{1,0:T(4,128)S(1)} fusion(f32[256,2304]{0,1:T(8,128)S(1)} %copy-done.2, f32[256]{0:T(256)S(1)} %bitcast.269, f32[256]{0:T(256)S(1)} %bitcast.260, f32[2304]{0:T(1024)S(1)} %get-tuple-element.410, f32[256]{0:T(256)S(1)} %bitcast.275, f32[256]{0:T(256)S(1)} %bitcast.263, f32[2304]{0:T(1024)S(1)} %get-tuple-element.409, ...), kind=kOutput, calls=%fused_computation.80.clone.1.clone | convolution fusion | flops 28901376 | bytes 2429956 | tf_op jit(solution)/shard_map/while/body/eval_jaxpr/dot_general | solution.py:64
  95.0 1.3 fusion.197
  96.3 4.9 %fusion.201 = f32[256,2304]{0,1:T(8,128)} fusion(f32[256]{0:T(256)S(1)} %bitcast.267, f32[256]{0:T(256)S(1)} %bitcast.258, f32[2304]{0:T(1024)S(1)} %get-tuple-element.410, f32[256]{0:T(256)S(1)} %bitcast.273, f32[256]{0:T(256)S(1)} %bitcast.261, f32[2304]{0:T(1024)S(1)} %get-tuple-element.409, f32[256]{0:T(256)S(1)} %bitcast.270, ...), kind=kOutput, calls=%fused_computation.66.clone.1.clone | convolution fusion | flops 1819738112 | bytes 2383872 | tf_op jit(solution)/shard_map/while/body/eval_jaxpr/dot_general | solution.py:103
  101.2 2.1 %fusion.200 = f32[256,2304]{0,1:T(8,128)S(1)} fusion(f32[3,4,2304]{2,1,0:T(4,128)S(1)} %get-tuple-element.469, s32[]{:T(128)} %get-tuple-element.460, f32[3,9,256]{2,1,0:T(8,128)S(1)} %get-tuple-element.468, s32[]{:T(128)S(6)} %add.599), kind=kOutput, calls=%fused_computation.88.clone.1.clone | convolution fusion | flops 21233664 | bytes 2401284 | tf_op jit(solution)/shard_map/while/body/eval_jaxpr/dot_general | solution.py:107
  103.4 4.4 %fusion.202 = f32[256,2304]{0,1:T(8,128)S(1)} fusion(f32[256,2304]{0,1:T(8,128)S(1)} %fusion.200, f32[256,2304]{0,1:T(8,128)S(1)} %copy-done.1, f32[2304]{0:T(1024)S(1)} %dynamic-slice_reduce_fusion.3, f32[256]{0:T(256)S(1)} %bitcast.268, f32[256]{0:T(256)S(1)} %bitcast.259, f32[2304]{0:T(1024)S(1)} %get-tuple-element.410, ...), kind=kOutput, calls=%fused_computation.70.clone.1.clone | convolution fusion | flops 1830944768 | bytes 7111680 | tf_op jit(solution)/shard_map/while/body/eval_jaxpr/dot_general | solution.py:114
  107.8 1.3 fusion.199
  111.6 2.2 %fusion.205 = f32[3,256]{1,0:T(4,128)S(1)} fusion(f32[256,2304]{0,1:T(8,128)S(1)} %copy-done.2, f32[256]{0:T(256)S(1)} %bitcast.269, f32[256]{0:T(256)S(1)} %bitcast.260, f32[2304]{0:T(1024)S(1)} %get-tuple-element.410, f32[256]{0:T(256)S(1)} %bitcast.275, f32[256]{0:T(256)S(1)} %bitcast.263, f32[2304]{0:T(1024)S(1)} %get-tuple-element.409, ...), kind=kOutput, calls=%fused_computation.80.clone.1.clone | convolution fusion | flops 28901376 | bytes 2429956 | tf_op jit(solution)/shard_map/while/body/eval_jaxpr/dot_general | solution.py:64
  114.9 2.7 %collective-permute-start.4 = (f32[16,9,256]{2,0,1:T(8,128)S(1)}, f32[16,9,256]{2,0,1:T(8,128)S(1)}, u32[]{:S(2)}, u32[]{:S(2)}) collective-permute-start(f32[16,9,256]{2,0,1:T(8,128)S(1)} %get-tuple-element.244), channel_id=1, source_target_pairs={{8,0},{12,4},{16,8},{20,12},{24,16},{28,20},{32,24},{36,28},{40,32... | collective-permute-start | bytes 442376 | tf_op jit(solution)/shard_map/ppermute | solution.py:15
  118.8 1.5 %collective-permute-done.4 = f32[16,9,256]{2,0,1:T(8,128)S(1)} collective-permute-done((f32[16,9,256]{2,0,1:T(8,128)S(1)}, f32[16,9,256]{2,0,1:T(8,128)S(1)}, u32[]{:S(2)}, u32[]{:S(2)}) %collective-permute-start.4) | collective-permute-done | bytes 147488 | tf_op jit(solution)/shard_map/ppermute | solution.py:15
  120.3 1.6 %collective-permute-done.5 = f32[16,9,256]{2,0,1:T(8,128)S(1)} collective-permute-done((f32[16,9,256]{2,0,1:T(8,128)S(1)}, f32[16,9,256]{2,0,1:T(8,128)S(1)}, u32[]{:S(2)}, u32[]{:S(2)}) %collective-permute-start.5) | collective-permute-done | bytes 147488 | tf_op jit(solution)/shard_map/ppermute | solution.py:15
  121.9 4.1 %collective-permute-done.6 = f32[16,9,256]{2,0,1:T(8,128)S(1)} collective-permute-done((f32[16,9,256]{2,0,1:T(8,128)S(1)}, f32[16,9,256]{2,0,1:T(8,128)S(1)}, u32[]{:S(2)}, u32[]{:S(2)}) %collective-permute-start.6) | collective-permute-done | bytes 147488 | tf_op jit(solution)/shard_map/ppermute | solution.py:15
  126.0 2.2 %collective-permute-done.7 = f32[16,9,256]{2,0,1:T(8,128)S(1)} collective-permute-done((f32[16,9,256]{2,0,1:T(8,128)S(1)}, f32[16,9,256]{2,0,1:T(8,128)S(1)}, u32[]{:S(2)}, u32[]{:S(2)}) %collective-permute-start.7) | collective-permute-done | bytes 147488 | tf_op jit(solution)/shard_map/ppermute | solution.py:15
  128.2 13.9 %all-gather = f32[64,9,256]{2,0,1:T(8,128)S(1)} all-gather(f32[16,9,256]{2,0,1:T(8,128)S(1)} %fusion.110), channel_id=2, replica_groups=mesh['cell'=64,'view'=4] {'view'}, dimensions={0}, use_global_device_ids=true | all-gather | bytes 737280 | tf_op jit(solution)/shard_map/all_gather | solution.py:187
  (95 shorter events, 15.0 us)
Async XLA Ops:
  1.6 15.5 %collective-permute-start = (f32[16,9,256]{2,1,0:T(8,128)S(1)}, f32[16,9,256]{2,1,0:T(8,128)S(1)}, u32[]{:S(2)}, u32[]{:S(2)}) collective-permute-start(f32[16,9,256]{2,1,0:T(8,128)S(1)} %copy.22), channel_id=1, source_target_pairs={{248,0},{252,4},{0,8},{4,12},{8,16},{12,20},{16,24},{20,28},{24,32... | collective-permute-start | bytes 442376 | tf_op jit(solution)/shard_map/ppermute | solution.py:15
  3.6 15.5 %collective-permute-start.1 = (f32[16,9,256]{2,1,0:T(8,128)S(1)}, f32[16,9,256]{2,1,0:T(8,128)S(1)}, u32[]{:S(2)}, u32[]{:S(2)}) collective-permute-start(f32[16,9,256]{2,1,0:T(8,128)S(1)} %copy.22), channel_id=1, source_target_pairs={{252,0},{0,4},{4,8},{8,12},{12,16},{16,20},{20,24},{24,28},{28,32}... | collective-permute-start | bytes 442376 | tf_op jit(solution)/shard_map/ppermute | solution.py:15
  3.6 17.9 %collective-permute-start.2 = (f32[16,9,256]{2,1,0:T(8,128)S(1)}, f32[16,9,256]{2,1,0:T(8,128)S(1)}, u32[]{:S(2)}, u32[]{:S(2)}) collective-permute-start(f32[16,9,256]{2,1,0:T(8,128)S(1)} %copy.22), channel_id=1, source_target_pairs={{4,0},{8,4},{12,8},{16,12},{20,16},{24,20},{28,24},{32,28},{36,32}... | collective-permute-start | bytes 442376 | tf_op jit(solution)/shard_map/ppermute | solution.py:15
  9.6 12.7 %collective-permute-start.3 = (f32[16,9,256]{2,1,0:T(8,128)S(1)}, f32[16,9,256]{2,1,0:T(8,128)S(1)}, u32[]{:S(2)}, u32[]{:S(2)}) collective-permute-start(f32[16,9,256]{2,1,0:T(8,128)S(1)} %copy.22), channel_id=1, source_target_pairs={{8,0},{12,4},{16,8},{20,12},{24,16},{28,20},{32,24},{36,28},{40,32... | collective-permute-start | bytes 442376 | tf_op jit(solution)/shard_map/ppermute | solution.py:15
  25.0 31.3 %copy-start = (f32[1,1,3,2304]{3,1,2,0:T(1,128)S(1)}, f32[1,1,3,2304]{3,1,2,0:T(1,128)}, u32[]{:S(2)}) copy-start(f32[1,1,3,2304]{3,1,2,0:T(1,128)} %param.15) | copy-start | bytes 82948
  63.0 2.2 %copy-start.1 = (f32[256,2304]{0,1:T(8,128)S(1)}, f32[256,2304]{0,1:T(8,128)}, u32[]{:S(2)}) copy-start(f32[256,2304]{0,1:T(8,128)} %fusion.201) | copy-start | bytes 7077892 | tf_op jit(solution)/shard_map/while
  71.8 1.7 %copy-start.2 = (f32[256,2304]{0,1:T(8,128)S(1)}, f32[256,2304]{0,1:T(8,128)}, u32[]{:S(2)}) copy-start(f32[256,2304]{0,1:T(8,128)} %fusion.201) | copy-start | bytes 7077892 | tf_op jit(solution)/shard_map/while
  82.1 2.2 %copy-start.1 = (f32[256,2304]{0,1:T(8,128)S(1)}, f32[256,2304]{0,1:T(8,128)}, u32[]{:S(2)}) copy-start(f32[256,2304]{0,1:T(8,128)} %fusion.201) | copy-start | bytes 7077892 | tf_op jit(solution)/shard_map/while
  90.9 1.7 %copy-start.2 = (f32[256,2304]{0,1:T(8,128)S(1)}, f32[256,2304]{0,1:T(8,128)}, u32[]{:S(2)}) copy-start(f32[256,2304]{0,1:T(8,128)} %fusion.201) | copy-start | bytes 7077892 | tf_op jit(solution)/shard_map/while
  101.2 2.2 %copy-start.1 = (f32[256,2304]{0,1:T(8,128)S(1)}, f32[256,2304]{0,1:T(8,128)}, u32[]{:S(2)}) copy-start(f32[256,2304]{0,1:T(8,128)} %fusion.201) | copy-start | bytes 7077892 | tf_op jit(solution)/shard_map/while
  110.0 1.7 %copy-start.2 = (f32[256,2304]{0,1:T(8,128)S(1)}, f32[256,2304]{0,1:T(8,128)}, u32[]{:S(2)}) copy-start(f32[256,2304]{0,1:T(8,128)} %fusion.201) | copy-start | bytes 7077892 | tf_op jit(solution)/shard_map/while
  114.9 5.4 %collective-permute-start.4 = (f32[16,9,256]{2,0,1:T(8,128)S(1)}, f32[16,9,256]{2,0,1:T(8,128)S(1)}, u32[]{:S(2)}, u32[]{:S(2)}) collective-permute-start(f32[16,9,256]{2,0,1:T(8,128)S(1)} %get-tuple-element.244), channel_id=1, source_target_pairs={{8,0},{12,4},{16,8},{20,12},{24,16},{28,20},{32,24},{36,28},{40,32... | collective-permute-start | bytes 442376 | tf_op jit(solution)/shard_map/ppermute | solution.py:15
  117.6 4.2 %collective-permute-start.5 = (f32[16,9,256]{2,0,1:T(8,128)S(1)}, f32[16,9,256]{2,0,1:T(8,128)S(1)}, u32[]{:S(2)}, u32[]{:S(2)}) collective-permute-start(f32[16,9,256]{2,0,1:T(8,128)S(1)} %get-tuple-element.247), channel_id=1, source_target_pairs={{4,0},{8,4},{12,8},{16,12},{20,16},{24,20},{28,24},{32,28},{36,32}... | collective-permute-start | bytes 442376 | tf_op jit(solution)/shard_map/ppermute | solution.py:15
  117.6 8.4 %collective-permute-start.6 = (f32[16,9,256]{2,0,1:T(8,128)S(1)}, f32[16,9,256]{2,0,1:T(8,128)S(1)}, u32[]{:S(2)}, u32[]{:S(2)}) collective-permute-start(f32[16,9,256]{2,0,1:T(8,128)S(1)} %get-tuple-element.246), channel_id=1, source_target_pairs={{252,0},{0,4},{4,8},{8,12},{12,16},{16,20},{20,24},{24,28},{28,32}... | collective-permute-start | bytes 442376 | tf_op jit(solution)/shard_map/ppermute | solution.py:15
  118.1 10.0 %collective-permute-start.7 = (f32[16,9,256]{2,0,1:T(8,128)S(1)}, f32[16,9,256]{2,0,1:T(8,128)S(1)}, u32[]{:S(2)}, u32[]{:S(2)}) collective-permute-start(f32[16,9,256]{2,0,1:T(8,128)S(1)} %get-tuple-element.245), channel_id=1, source_target_pairs={{248,0},{252,4},{0,8},{4,12},{8,16},{12,20},{16,24},{20,28},{24,32... | collective-permute-start | bytes 442376 | tf_op jit(solution)/shard_map/ppermute | solution.py:15
